TPU v7x, 32 devices: a whole 2x2x4 slice. The times are simulated.
32 devices in a mesh: dp: 8 (over z, core), fsdp: 4 (over y, x).
Axes of the slice: x: 2, y: 2, z: 4, core: 2. Of those that a mesh axis runs over, the one named last changes fastest.
Arguments:
- tokens: bfloat16 [32768, 768], P(('dp', 'fsdp')), may hold values from -6 to 6
- latents: bfloat16 [1024, 768], P(('dp', 'fsdp')), may hold values from -6 to 6
- valid_mask: int32 [32768], P(('dp', 'fsdp')), may hold values from 0 to 1, as said below
- out_cotangent: bfloat16 [32768, 768], P(('dp', 'fsdp')), may hold values from -6 to 6
- latent_cotangent: bfloat16 [1024, 768], P(('dp', 'fsdp')), may hold values from -6 to 6
- norm_gains: bfloat16 [8, 768], P(None, ('dp', 'fsdp')), may hold values from 0.5 to 1.5
- local_qkv: bfloat16 [2304, 768], P(('dp', 'fsdp')), may hold values from -0.21875 to 0.21875
- local_out: bfloat16 [768, 768], P(('dp', 'fsdp')), may hold values from -0.875 to 0.875
- token_up: bfloat16 [3072, 768], P(('dp', 'fsdp')), may hold values from -0.21875 to 0.21875
- token_down: bfloat16 [768, 3072], P(('dp', 'fsdp')), may hold values from -0.109375 to 0.109375
- read_qkv: bfloat16 [2304, 768], P(('dp', 'fsdp')), may hold values from -0.21875 to 0.21875
- read_out: bfloat16 [768, 768], P(('dp', 'fsdp')), may hold values from -0.875 to 0.875
- global_qkv: bfloat16 [2304, 768], P(('dp', 'fsdp')), may hold values from -0.21875 to 0.21875
- global_out: bfloat16 [768, 768], P(('dp', 'fsdp')), may hold values from -0.625 to 0.625
- latent_up: bfloat16 [3072, 768], P(('dp', 'fsdp')), may hold values from -0.21875 to 0.21875
- latent_down: bfloat16 [768, 3072], P(('dp', 'fsdp')), may hold values from -0.109375 to 0.109375
- write_qkv: bfloat16 [2304, 768], P(('dp', 'fsdp')), may hold values from -0.21875 to 0.21875
- write_out: bfloat16 [768, 768], P(('dp', 'fsdp')), may hold values from -0.3125 to 0.3125
Outputs:
- out_tokens: bfloat16 [32768, 768], P(('dp', 'fsdp'))
- out_latents: bfloat16 [1024, 768], P(('dp', 'fsdp'))
- grad_tokens: float32 [32768, 768], P(('dp', 'fsdp'))
- grad_latents: float32 [1024, 768], P(('dp', 'fsdp'))
- grad_norm_gains: float32 [8, 768], P(None, ('dp', 'fsdp'))
- grad_local_qkv: float32 [2304, 768], P(('dp', 'fsdp'))
- grad_local_out: float32 [768, 768], P(('dp', 'fsdp'))
- grad_token_up: float32 [3072, 768], P(('dp', 'fsdp'))
- grad_token_down: float32 [768, 3072], P(('dp', 'fsdp'))
- grad_read_qkv: float32 [2304, 768], P(('dp', 'fsdp'))
- grad_read_out: float32 [768, 768], P(('dp', 'fsdp'))
- grad_global_qkv: float32 [2304, 768], P(('dp', 'fsdp'))
- grad_global_out: float32 [768, 768], P(('dp', 'fsdp'))
- grad_latent_up: float32 [3072, 768], P(('dp', 'fsdp'))
- grad_latent_down: float32 [768, 3072], P(('dp', 'fsdp'))
- grad_write_qkv: float32 [2304, 768], P(('dp', 'fsdp'))
- grad_write_out: float32 [768, 768], P(('dp', 'fsdp'))
Inputs may be any that keep to these rules, and one draw needn't show every extreme that they name: `valid_mask`: within each image of 4096 consecutive slots the valid slots come first and number at least 3841, so every group holds a valid slot.
All inputs are finite; a program needn't handle non-finite values.
Results may differ from a plain program's by a relative error of at most 0.02.
Values may be sent and summed in bfloat16 or wider, within the bound.
A program may use at most 320 MiB of HBM per device.

v0:
```python
import jax
import jax.numpy as jnp
from jax import lax
from jax.sharding import PartitionSpec as P

HDIM = 64
GROUP = 256
LAT = 8
SLOTS = 4096


norm_eps = 1e-05
mask_fill = -1000000000.0


def project(row_block, weight):
    return lax.dot_general(
        row_block,
        weight,
        (((row_block.ndim - 1,), (1,)), ((), ())),
        preferred_element_type=jnp.float32,
    )


def back_project(grad_rows, weight):
    return lax.dot_general(
        grad_rows,
        weight,
        (((grad_rows.ndim - 1,), (0,)), ((), ())),
        preferred_element_type=jnp.float32,
    )


def weight_grad(grad_rows, in_rows):
    grad_flat = grad_rows.reshape(-1, grad_rows.shape[-1])
    in_flat = in_rows.reshape(-1, in_rows.shape[-1])
    return lax.dot_general(
        grad_flat, in_flat, (((0,), (0,)), ((), ())), preferred_element_type=jnp.float32
    )


def layer_norm(values, gain_row):
    centered = values - jnp.mean(values, axis=-1, keepdims=True)
    variance = jnp.mean(centered * centered, axis=-1, keepdims=True)
    return centered * lax.rsqrt(variance + norm_eps) * gain_row


def norm_back(values, gain_row, grad_rows):
    normed, pullback = jax.vjp(layer_norm, values, gain_row)
    return pullback(grad_rows)


def gelu_tanh(values):
    return jax.nn.gelu(values, approximate=True)


def split_heads(values):
    return values.reshape(values.shape[:-1] + (values.shape[-1] // HDIM, HDIM))


def scores_of(query_bf, key_bf, key_bias):
    raw_scores = jnp.einsum(
        "bqhe,bkhe->bhqk",
        split_heads(query_bf),
        split_heads(key_bf),
        preferred_element_type=jnp.float32,
    )
    return raw_scores * HDIM ** (-0.5) + key_bias[:, None, :, :]


def attend(query_bf, key_bf, value_bf, key_bias):
    scores = scores_of(query_bf, key_bf, key_bias)
    row_max = jnp.max(scores, axis=-1, keepdims=True)
    exponent = jnp.exp(scores - row_max)
    row_sum = jnp.sum(exponent, axis=-1, keepdims=True)
    probs_low = (exponent / row_sum).astype(jnp.bfloat16)
    mixed = jnp.einsum(
        "bhqk,bkhe->bqhe", probs_low, split_heads(value_bf), preferred_element_type=jnp.float32
    )
    return (mixed.reshape(query_bf.shape).astype(jnp.bfloat16), row_max + jnp.log(row_sum))


def attend_back(query_bf, key_bf, value_bf, key_bias, log_total, grad_mixed):
    scores = scores_of(query_bf, key_bf, key_bias)
    probs_full = jnp.exp(scores - log_total)
    probs_low = probs_full.astype(jnp.bfloat16)
    value_heads = split_heads(value_bf)
    grad_heads = split_heads(grad_mixed)
    mixed = jnp.einsum(
        "bhqk,bkhe->bqhe", probs_low, value_heads, preferred_element_type=jnp.float32
    )
    mixed = mixed.reshape(query_bf.shape).astype(jnp.bfloat16)
    grad_probs = jnp.einsum(
        "bqhe,bkhe->bhqk", grad_heads, value_heads, preferred_element_type=jnp.float32
    )
    grad_scores = probs_full * (
        grad_probs - jnp.sum(grad_probs * probs_full, axis=-1, keepdims=True)
    )
    grad_scores = grad_scores.astype(jnp.bfloat16)
    score_scale = HDIM ** (-0.5)
    grad_query = (
        jnp.einsum(
            "bhqk,bkhe->bqhe", grad_scores, split_heads(key_bf), preferred_element_type=jnp.float32
        )
        * score_scale
    )
    grad_key = (
        jnp.einsum(
            "bhqk,bqhe->bkhe",
            grad_scores,
            split_heads(query_bf),
            preferred_element_type=jnp.float32,
        )
        * score_scale
    )
    grad_value = jnp.einsum(
        "bhqk,bqhe->bkhe", probs_low, grad_heads, preferred_element_type=jnp.float32
    )
    return (
        mixed,
        grad_query.reshape(query_bf.shape),
        grad_key.reshape(key_bf.shape),
        grad_value.reshape(value_bf.shape),
    )


def queries_keys(query_norm, key_norm, qkv_weight):
    model_width = query_norm.shape[-1]
    query_bf = project(query_norm, qkv_weight[:model_width]).astype(jnp.bfloat16)
    key_values = project(key_norm, qkv_weight[model_width:]).astype(jnp.bfloat16)
    return (query_bf, key_values)


def block_attention(query_norm, key_norm, qkv_weight, out_weight, key_bias):
    model_width = query_norm.shape[-1]
    query_bf, key_values = queries_keys(query_norm, key_norm, qkv_weight)
    mixed, log_total = attend(
        query_bf, key_values[..., :model_width], key_values[..., model_width:], key_bias
    )
    return (project(mixed, out_weight), log_total)


def block_attention_back(
    query_norm, key_norm, qkv_weight, out_weight, key_bias, log_total, grad_branch
):
    model_width = query_norm.shape[-1]
    query_bf, key_values = queries_keys(query_norm, key_norm, qkv_weight)
    branch_bf = grad_branch.astype(jnp.bfloat16)
    grad_mixed = back_project(branch_bf, out_weight).astype(jnp.bfloat16)
    mixed, grad_query, grad_key, grad_value = attend_back(
        query_bf,
        key_values[..., :model_width],
        key_values[..., model_width:],
        key_bias,
        log_total,
        grad_mixed,
    )
    query_grad_bf = grad_query.astype(jnp.bfloat16)
    keyval_grad_bf = jnp.concatenate([grad_key, grad_value], axis=-1).astype(jnp.bfloat16)
    grad_qkv = jnp.concatenate(
        [weight_grad(query_grad_bf, query_norm), weight_grad(keyval_grad_bf, key_norm)], axis=0
    )
    grad_out = weight_grad(branch_bf, mixed)
    grad_query_norm = back_project(query_grad_bf, qkv_weight[:model_width])
    grad_key_norm = back_project(keyval_grad_bf, qkv_weight[model_width:])
    return (grad_query_norm, grad_key_norm, grad_qkv, grad_out)


def mlp_forward(norm_rows, up_weight, down_weight):
    hidden_pre = project(norm_rows, up_weight)
    activated = gelu_tanh(hidden_pre).astype(jnp.bfloat16)
    return project(activated, down_weight)


def mlp_back(norm_rows, up_weight, down_weight, grad_branch):
    hidden_pre = project(norm_rows, up_weight)
    activated, pullback = jax.vjp(gelu_tanh, hidden_pre)
    act_bf = activated.astype(jnp.bfloat16)
    branch_bf = grad_branch.astype(jnp.bfloat16)
    grad_act = back_project(branch_bf, down_weight)
    grad_pre = pullback(grad_act)[0].astype(jnp.bfloat16)
    return (
        back_project(grad_pre, up_weight),
        weight_grad(grad_pre, norm_rows),
        weight_grad(branch_bf, act_bf),
    )


def shards(
    tokens,
    latents,
    valid_mask,
    out_cotangent,
    latent_cotangent,
    norm_gains,
    local_qkv,
    local_out,
    token_up,
    token_down,
    read_qkv,
    read_out,
    global_qkv,
    global_out,
    latent_up,
    latent_down,
    write_qkv,
    write_out,
):
    model_width = tokens.shape[1]
    group_count = tokens.shape[0] // GROUP
    latent_count = group_count * LAT
    per_image = SLOTS // GROUP
    valid_rows = valid_mask.astype(jnp.float32)
    token_bias = (
        jnp.where(valid_mask > 0, 0.0, mask_fill).astype(jnp.float32).reshape(group_count, 1, GROUP)
    )
    local_image = (
        lax.axis_index("fsdp") * group_count + jnp.arange(latent_count, dtype=jnp.int32) // LAT
    ) // per_image
    remote_image = jnp.arange(lax.axis_size("fsdp") * latent_count, dtype=jnp.int32) // (
        LAT * per_image
    )
    latent_bias = jnp.where(local_image[:, None] == remote_image[None, :], 0.0, mask_fill).astype(
        jnp.float32
    )[None]
    empty_bias = jnp.zeros((group_count, 1, LAT), jnp.float32)
    token_side = (
        lax.all_gather(local_qkv, ("dp", "fsdp"), axis=0, tiled=True),
        lax.all_gather(local_out, ("dp", "fsdp"), axis=0, tiled=True),
        lax.all_gather(token_up, ("dp", "fsdp"), axis=0, tiled=True),
        lax.all_gather(token_down, ("dp", "fsdp"), axis=0, tiled=True),
        lax.all_gather(norm_gains, ("dp", "fsdp"), axis=1, tiled=True),
    )
    latent_side = (
        lax.all_gather(read_qkv, ("dp", "fsdp"), axis=0, tiled=True),
        lax.all_gather(read_out, ("dp", "fsdp"), axis=0, tiled=True),
        lax.all_gather(global_qkv, ("dp", "fsdp"), axis=0, tiled=True),
        lax.all_gather(global_out, ("dp", "fsdp"), axis=0, tiled=True),
        lax.all_gather(latent_up, ("dp", "fsdp"), axis=0, tiled=True),
        lax.all_gather(latent_down, ("dp", "fsdp"), axis=0, tiled=True),
        lax.all_gather(write_qkv, ("dp", "fsdp"), axis=0, tiled=True),
        lax.all_gather(write_out, ("dp", "fsdp"), axis=0, tiled=True),
    )
    gain_rows = token_side[4].astype(jnp.float32)
    residual_in = tokens.astype(jnp.float32).reshape(group_count, GROUP, model_width)
    local_norm = layer_norm(residual_in, gain_rows[0]).astype(jnp.bfloat16)
    branch, local_total = block_attention(
        local_norm, local_norm, token_side[0], token_side[1], token_bias
    )
    residual_one = residual_in + branch
    token_norm = layer_norm(residual_one, gain_rows[1]).astype(jnp.bfloat16)
    residual_two = residual_one + mlp_forward(token_norm, token_side[2], token_side[3])
    latent_in = latents.astype(jnp.float32).reshape(group_count, LAT, model_width)
    read_query = layer_norm(latent_in, gain_rows[2]).astype(jnp.bfloat16)
    read_keys = layer_norm(residual_two, gain_rows[3]).astype(jnp.bfloat16)
    branch, read_total = block_attention(
        read_query, read_keys, latent_side[0], latent_side[1], token_bias
    )
    latent_one = (latent_in + branch).reshape(latent_count, model_width)
    global_norm = layer_norm(latent_one, gain_rows[4]).astype(jnp.bfloat16)
    global_query, global_keyval = queries_keys(global_norm, global_norm, latent_side[2])
    gathered = lax.all_gather(global_keyval, "fsdp", axis=0, tiled=True)
    global_mixed, global_total = attend(
        global_query[None],
        gathered[None, :, :model_width],
        gathered[None, :, model_width:],
        latent_bias,
    )
    latent_two = latent_one + project(global_mixed[0], latent_side[3])
    latent_norm = layer_norm(latent_two, gain_rows[5]).astype(jnp.bfloat16)
    latent_out = latent_two + mlp_forward(latent_norm, latent_side[4], latent_side[5])
    latent_groups = latent_out.reshape(group_count, LAT, model_width)
    write_query = layer_norm(residual_two, gain_rows[6]).astype(jnp.bfloat16)
    write_keys = layer_norm(latent_groups, gain_rows[7]).astype(jnp.bfloat16)
    branch, write_total = block_attention(
        write_query, write_keys, latent_side[6], latent_side[7], empty_bias
    )
    residual_out = residual_two + branch
    mask_rows = valid_rows.reshape(group_count, GROUP, 1)
    out_tokens = (residual_out * mask_rows).reshape(-1, model_width).astype(jnp.bfloat16)
    out_latents = latent_out.astype(jnp.bfloat16)
    back_all = (token_side[0], token_side[1], token_side[2], token_side[3]) + tuple(latent_side)
    grad_residual_out = (
        out_cotangent.astype(jnp.float32).reshape(group_count, GROUP, model_width) * mask_rows
    )
    grad_latent_out = latent_cotangent.astype(jnp.float32)
    grad_query_norm, grad_key_norm, write_qkv_grad, write_out_grad = block_attention_back(
        write_query,
        write_keys,
        back_all[10],
        back_all[11],
        empty_bias,
        write_total,
        grad_residual_out,
    )
    grad_values, grad_gain_six = norm_back(residual_two, gain_rows[6], grad_query_norm)
    grad_residual_two = grad_residual_out + grad_values
    grad_values, grad_gain_seven = norm_back(latent_groups, gain_rows[7], grad_key_norm)
    grad_latent_out = grad_latent_out + grad_values.reshape(latent_count, model_width)
    grad_norm_rows, latent_up_grad, latent_down_grad = mlp_back(
        latent_norm, back_all[8], back_all[9], grad_latent_out
    )
    grad_values, grad_gain_five = norm_back(latent_two, gain_rows[5], grad_norm_rows)
    grad_latent_two = grad_latent_out + grad_values
    branch_bf = grad_latent_two.astype(jnp.bfloat16)
    grad_mixed = back_project(branch_bf, back_all[7]).astype(jnp.bfloat16)
    mixed_again, grad_query, grad_key, grad_value = attend_back(
        global_query[None],
        gathered[None, :, :model_width],
        gathered[None, :, model_width:],
        latent_bias,
        global_total,
        grad_mixed[None],
    )
    own_key, own_value = (
        lax.psum_scatter(
            grad_key[0].astype(jnp.bfloat16), "fsdp", scatter_dimension=0, tiled=True
        ).astype(jnp.float32),
        lax.psum_scatter(
            grad_value[0].astype(jnp.bfloat16), "fsdp", scatter_dimension=0, tiled=True
        ).astype(jnp.float32),
    )
    query_grad_bf = grad_query[0].astype(jnp.bfloat16)
    keyval_grad_bf = jnp.concatenate([own_key, own_value], axis=-1).astype(jnp.bfloat16)
    global_qkv_grad = jnp.concatenate(
        [weight_grad(query_grad_bf, global_norm), weight_grad(keyval_grad_bf, global_norm)], axis=0
    )
    global_out_grad = weight_grad(branch_bf, mixed_again[0])
    grad_norm_rows = back_project(query_grad_bf, back_all[6][:model_width]) + back_project(
        keyval_grad_bf, back_all[6][model_width:]
    )
    grad_values, grad_gain_four = norm_back(latent_one, gain_rows[4], grad_norm_rows)
    grad_latent_one = (grad_latent_two + grad_values).reshape(group_count, LAT, model_width)
    grad_query_norm, grad_key_norm, read_qkv_grad, read_out_grad = block_attention_back(
        read_query, read_keys, back_all[4], back_all[5], token_bias, read_total, grad_latent_one
    )
    grad_values, grad_gain_two = norm_back(latent_in, gain_rows[2], grad_query_norm)
    grad_latent_in = grad_latent_one + grad_values
    grad_values, grad_gain_three = norm_back(residual_two, gain_rows[3], grad_key_norm)
    grad_residual_two = grad_residual_two + grad_values
    grad_norm_rows, token_up_grad, token_down_grad = mlp_back(
        token_norm, back_all[2], back_all[3], grad_residual_two
    )
    grad_values, grad_gain_one = norm_back(residual_one, gain_rows[1], grad_norm_rows)
    grad_residual_one = grad_residual_two + grad_values
    grad_query_norm, grad_key_norm, local_qkv_grad, local_out_grad = block_attention_back(
        local_norm, local_norm, back_all[0], back_all[1], token_bias, local_total, grad_residual_one
    )
    grad_values, grad_gain_zero = norm_back(
        residual_in, gain_rows[0], grad_query_norm + grad_key_norm
    )
    grad_residual_in = grad_residual_one + grad_values
    gain_grads = jnp.stack(
        [
            grad_gain_zero,
            grad_gain_one,
            grad_gain_two,
            grad_gain_three,
            grad_gain_four,
            grad_gain_five,
            grad_gain_six,
            grad_gain_seven,
        ]
    )
    summed = (
        lax.psum_scatter(local_qkv_grad, ("dp", "fsdp"), scatter_dimension=0, tiled=True),
        lax.psum_scatter(local_out_grad, ("dp", "fsdp"), scatter_dimension=0, tiled=True),
        lax.psum_scatter(token_up_grad, ("dp", "fsdp"), scatter_dimension=0, tiled=True),
        lax.psum_scatter(token_down_grad, ("dp", "fsdp"), scatter_dimension=0, tiled=True),
        lax.psum_scatter(read_qkv_grad, ("dp", "fsdp"), scatter_dimension=0, tiled=True),
        lax.psum_scatter(read_out_grad, ("dp", "fsdp"), scatter_dimension=0, tiled=True),
        lax.psum_scatter(global_qkv_grad, ("dp", "fsdp"), scatter_dimension=0, tiled=True),
        lax.psum_scatter(global_out_grad, ("dp", "fsdp"), scatter_dimension=0, tiled=True),
        lax.psum_scatter(latent_up_grad, ("dp", "fsdp"), scatter_dimension=0, tiled=True),
        lax.psum_scatter(latent_down_grad, ("dp", "fsdp"), scatter_dimension=0, tiled=True),
        lax.psum_scatter(write_qkv_grad, ("dp", "fsdp"), scatter_dimension=0, tiled=True),
        lax.psum_scatter(write_out_grad, ("dp", "fsdp"), scatter_dimension=0, tiled=True),
        lax.psum_scatter(gain_grads, ("dp", "fsdp"), scatter_dimension=1, tiled=True),
    )
    weight_sums = tuple(summed[:12])
    gain_sum = summed[12]
    return (
        out_tokens,
        out_latents,
        grad_residual_in.reshape(-1, model_width),
        grad_latent_in.reshape(-1, model_width),
        gain_sum,
        weight_sums[0],
        weight_sums[1],
        weight_sums[2],
        weight_sums[3],
        weight_sums[4],
        weight_sums[5],
        weight_sums[6],
        weight_sums[7],
        weight_sums[8],
        weight_sums[9],
        weight_sums[10],
        weight_sums[11],
    )


def solution(mesh):
    in_specs = (
        P(("dp", "fsdp"), None),
        P(("dp", "fsdp"), None),
        P(("dp", "fsdp")),
        P(("dp", "fsdp"), None),
        P(("dp", "fsdp"), None),
        P(None, ("dp", "fsdp")),
        P(("dp", "fsdp"), None),
        P(("dp", "fsdp"), None),
        P(("dp", "fsdp"), None),
        P(("dp", "fsdp"), None),
        P(("dp", "fsdp"), None),
        P(("dp", "fsdp"), None),
        P(("dp", "fsdp"), None),
        P(("dp", "fsdp"), None),
        P(("dp", "fsdp"), None),
        P(("dp", "fsdp"), None),
        P(("dp", "fsdp"), None),
        P(("dp", "fsdp"), None),
    )
    out_specs = (
        P(("dp", "fsdp"), None),
        P(("dp", "fsdp"), None),
        P(("dp", "fsdp"), None),
        P(("dp", "fsdp"), None),
        P(None, ("dp", "fsdp")),
        P(("dp", "fsdp"), None),
        P(("dp", "fsdp"), None),
        P(("dp", "fsdp"), None),
        P(("dp", "fsdp"), None),
        P(("dp", "fsdp"), None),
        P(("dp", "fsdp"), None),
        P(("dp", "fsdp"), None),
        P(("dp", "fsdp"), None),
        P(("dp", "fsdp"), None),
        P(("dp", "fsdp"), None),
        P(("dp", "fsdp"), None),
        P(("dp", "fsdp"), None),
    )
    return jax.shard_map(shards, mesh=mesh, in_specs=in_specs, out_specs=out_specs, check_vma=False)
```

profile of v0, /device:TPU:0, one launch (start us, length us, event | category | flops | bytes accessed | tf_op | source)
XLA Modules:
  0.0 2337.7 jit_solution(13829050877021799556)
XLA Ops:
  23.0 70.3 %all-gather = bf16[32,24,8]{1,2,0:T(8,128)(2,1)S(1)} all-gather(bf16[1,24,8]{1,2,0:T(8,128)(2,1)S(1)} %bitcast.392), channel_id=1, replica_groups=mesh['dp'=8,'fsdp'=4] {'dp','fsdp'}, dimensions={0}, use_global_device_ids=true | all-gather | bytes 12672 | tf_op jit(solution)/shard_map/all_gather | solution.py:232
  100.8 28.9 %all-gather.22.cloned.1.call-done = bf16[2304,768]{1,0:T(8,128)(2,1)} async-done(((bf16[72,768]{1,0:T(8,128)(2,1)}), bf16[2304,768]{1,0:T(8,128)(2,1)}) %all-gather.22.cloned.1.call-update) | async-done | bytes 3538960 | tf_op jit(solution)/shard_map/all_gather | solution.py:235
  131.7 59.9 %all-gather.14.cloned.1.call-done = bf16[2304,768]{1,0:T(8,128)(2,1)} async-done(((bf16[72,768]{1,0:T(8,128)(2,1)}), bf16[2304,768]{1,0:T(8,128)(2,1)}) %all-gather.14.cloned.1.call-update) | async-done | bytes 3538960 | tf_op jit(solution)/shard_map/all_gather | solution.py:228
  222.2 25.0 %all-gather.16.cloned.1.call-done = bf16[768,768]{1,0:T(8,128)(2,1)} async-done(((bf16[24,768]{1,0:T(8,128)(2,1)}), bf16[768,768]{1,0:T(8,128)(2,1)}) %all-gather.16.cloned.1.call-update) | async-done | bytes 1179664 | tf_op jit(solution)/shard_map/all_gather | solution.py:229
  252.3 60.2 %all-gather.18.cloned.1.call-done = bf16[3072,768]{1,0:T(8,128)(2,1)} async-done(((bf16[96,768]{1,0:T(8,128)(2,1)}), bf16[3072,768]{1,0:T(8,128)(2,1)}) %all-gather.18.cloned.1.call-update) | async-done | bytes 4718608 | tf_op jit(solution)/shard_map/all_gather | solution.py:230
  312.5 10.9 fusion.17
  323.4 54.2 %all-gather.20.cloned.1.call-done = bf16[768,3072]{1,0:T(8,128)(2,1)} async-done(((bf16[24,3072]{1,0:T(8,128)(2,1)}), bf16[768,3072]{1,0:T(8,128)(2,1)}) %all-gather.20.cloned.1.call-update) | async-done | bytes 4718608 | tf_op jit(solution)/shard_map/all_gather | solution.py:231
  377.7 12.4 fusion.182
  390.6 48.9 %all-gather.34.cloned.1.call-done = bf16[2304,768]{1,0:T(8,128)(2,1)} async-done(((bf16[72,768]{1,0:T(8,128)(2,1)}), bf16[2304,768]{1,0:T(8,128)(2,1)}) %all-gather.34.cloned.1.call-update) | async-done | bytes 3538960 | tf_op jit(solution)/shard_map/all_gather | solution.py:241
  462.6 32.7 %all-gather.24.cloned.1.call-done = bf16[768,768]{1,0:T(8,128)(2,1)} async-done(((bf16[24,768]{1,0:T(8,128)(2,1)}), bf16[768,768]{1,0:T(8,128)(2,1)}) %all-gather.24.cloned.1.call-update) | async-done | bytes 1179664 | tf_op jit(solution)/shard_map/all_gather | solution.py:236
  499.2 58.1 %all-gather.26.cloned.1.call-done = bf16[2304,768]{1,0:T(8,128)(2,1)} async-done(((bf16[72,768]{1,0:T(8,128)(2,1)}), bf16[2304,768]{1,0:T(8,128)(2,1)}) %all-gather.26.cloned.1.call-update) | async-done | bytes 3538960 | tf_op jit(solution)/shard_map/all_gather | solution.py:237
  562.3 9.6 all_gather.50
  580.3 32.6 %all-gather.28.cloned.1.call-done = bf16[768,768]{1,0:T(8,128)(2,1)} async-done(((bf16[24,768]{1,0:T(8,128)(2,1)}), bf16[768,768]{1,0:T(8,128)(2,1)}) %all-gather.28.cloned.1.call-update) | async-done | bytes 1179664 | tf_op jit(solution)/shard_map/all_gather | solution.py:238
  616.9 61.4 %all-gather.30.cloned.1.call-done = bf16[3072,768]{1,0:T(8,128)(2,1)} async-done(((bf16[96,768]{1,0:T(8,128)(2,1)}), bf16[3072,768]{1,0:T(8,128)(2,1)}) %all-gather.30.cloned.1.call-update) | async-done | bytes 4718608 | tf_op jit(solution)/shard_map/all_gather | solution.py:239
  682.2 61.2 %all-gather.32.cloned.1.call-done = bf16[768,3072]{1,0:T(8,128)(2,1)} async-done(((bf16[24,3072]{1,0:T(8,128)(2,1)}), bf16[768,3072]{1,0:T(8,128)(2,1)}) %all-gather.32.cloned.1.call-update) | async-done | bytes 4718608 | tf_op jit(solution)/shard_map/all_gather | solution.py:240
  808.5 9.1 convolution_convert_fusion.5
  832.9 13.7 reduce-scatter.46.cloned.1.call-done
  886.3 17.4 fusion.6
  967.7 8.5 multiply_reduce_fusion
  1016.4 10.8 convolution_bitcast_fusion.1
  1027.3 11.7 convolution_bitcast_fusion
  1056.5 39.6 %all-reduce = f32[8,768]{1,0:T(8,128)S(1)} all-reduce(f32[8,768]{1,0:T(8,128)S(1)} %stack.29), channel_id=4, replica_groups=mesh['dp'=8,'fsdp'=4] {'dp','fsdp'}, use_global_device_ids=true, to_apply=%region_52.53.clone | all-reduce | flops 6144 | bytes 49152
  1103.1 56.8 %reduce-scatter.22.cloned.1.call-done = f32[24,768]{1,0:T(8,128)} async-done(((f32[768,768]{1,0:T(8,128)}), f32[24,768]{1,0:T(8,128)}) %reduce-scatter.22.cloned.1.call-update) | async-done | bytes 73744 | tf_op jit(solution)/shard_map/reduce_scatter | solution.py:367
  1159.9 104.7 %reduce-scatter.30.cloned.1.call-done = f32[24,768]{1,0:T(8,128)} async-done(((f32[768,768]{1,0:T(8,128)}), f32[24,768]{1,0:T(8,128)}) %reduce-scatter.30.cloned.1.call-update) | async-done | bytes 73744 | tf_op jit(solution)/shard_map/reduce_scatter | solution.py:371
  1264.5 124.4 %reduce-scatter.40.cloned.1.call-done = f32[72,768]{1,0:T(8,128)} async-done(((f32[2304,768]{1,0:T(8,128)}), f32[72,768]{1,0:T(8,128)}) %reduce-scatter.40.cloned.1.call-update) | async-done | bytes 221200 | tf_op jit(solution)/shard_map/reduce_scatter | solution.py:376
  1388.9 125.3 %reduce-scatter.28.cloned.1.call-done = f32[72,768]{1,0:T(8,128)} async-done(((f32[2304,768]{1,0:T(8,128)}), f32[72,768]{1,0:T(8,128)}) %reduce-scatter.28.cloned.1.call-update) | async-done | bytes 221200 | tf_op jit(solution)/shard_map/reduce_scatter | solution.py:370
  1514.3 124.8 %reduce-scatter.32.cloned.1.call-done = f32[72,768]{1,0:T(8,128)} async-done(((f32[2304,768]{1,0:T(8,128)}), f32[72,768]{1,0:T(8,128)}) %reduce-scatter.32.cloned.1.call-update) | async-done | bytes 221200 | tf_op jit(solution)/shard_map/reduce_scatter | solution.py:372
  1639.1 125.6 %reduce-scatter.20.cloned.1.call-done = f32[72,768]{1,0:T(8,128)} async-done(((f32[2304,768]{1,0:T(8,128)}), f32[72,768]{1,0:T(8,128)}) %reduce-scatter.20.cloned.1.call-update) | async-done | bytes 221200 | tf_op jit(solution)/shard_map/reduce_scatter | solution.py:366
  1764.7 141.4 %reduce-scatter.38.cloned.1.call-done = f32[24,3072]{1,0:T(8,128)} async-done(((f32[768,3072]{1,0:T(8,128)}), f32[24,3072]{1,0:T(8,128)}) %reduce-scatter.38.cloned.1.call-update) | async-done | bytes 294928 | tf_op jit(solution)/shard_map/reduce_scatter | solution.py:375
  1906.1 141.9 %reduce-scatter.36.cloned.1.call-done = f32[96,768]{1,0:T(8,128)} async-done(((f32[3072,768]{1,0:T(8,128)}), f32[96,768]{1,0:T(8,128)}) %reduce-scatter.36.cloned.1.call-update) | async-done | bytes 294928 | tf_op jit(solution)/shard_map/reduce_scatter | solution.py:374
  2048.1 141.1 %reduce-scatter.24.cloned.1.call-done = f32[96,768]{1,0:T(8,128)} async-done(((f32[3072,768]{1,0:T(8,128)}), f32[96,768]{1,0:T(8,128)}) %reduce-scatter.24.cloned.1.call-update) | async-done | bytes 294928 | tf_op jit(solution)/shard_map/reduce_scatter | solution.py:368
  2189.2 141.8 %reduce-scatter.26.cloned.1.call-done = f32[24,3072]{1,0:T(8,128)} async-done(((f32[768,3072]{1,0:T(8,128)}), f32[24,3072]{1,0:T(8,128)}) %reduce-scatter.26.cloned.1.call-update) | async-done | bytes 294928 | tf_op jit(solution)/shard_map/reduce_scatter | solution.py:369
  (627 shorter events, 356.2 us)
Async XLA Ops:
  7.2 87.2 %all-gather.36.cloned.1.call-start = ((), (), s32[]{:S(2)}) async-start(), calls=%async_computation.25 | async-start | bytes 1216512 | tf_op jit(solution)/shard_map/all_gather | solution.py:242
  8.0 121.8 %all-gather.22.cloned.1.call-start = ((), (), s32[]{:S(2)}) async-start(), calls=%async_computation.18 | async-start | bytes 3649536 | tf_op jit(solution)/shard_map/all_gather | solution.py:235
  8.7 182.9 %all-gather.14.cloned.1.call-start = ((), (), s32[]{:S(2)}) async-start(), calls=%async_computation.14 | async-start | bytes 3649536 | tf_op jit(solution)/shard_map/all_gather | solution.py:228
  9.4 237.8 %all-gather.16.cloned.1.call-start = ((), (), s32[]{:S(2)}) async-start(), calls=%async_computation.15 | async-start | bytes 1216512 | tf_op jit(solution)/shard_map/all_gather | solution.py:229
  10.0 302.5 %all-gather.18.cloned.1.call-start = ((), (), s32[]{:S(2)}) async-start(), calls=%async_computation.16 | async-start | bytes 4866048 | tf_op jit(solution)/shard_map/all_gather | solution.py:230
  10.6 367.0 %all-gather.20.cloned.1.call-start = ((), (), s32[]{:S(2)}) async-start(), calls=%async_computation.17 | async-start | bytes 4866048 | tf_op jit(solution)/shard_map/all_gather | solution.py:231
  11.2 428.3 %all-gather.34.cloned.1.call-start = ((), (), s32[]{:S(2)}) async-start(), calls=%async_computation.24 | async-start | bytes 3649536 | tf_op jit(solution)/shard_map/all_gather | solution.py:241
  11.9 483.4 %all-gather.24.cloned.1.call-start = ((), (), s32[]{:S(2)}) async-start(), calls=%async_computation.19 | async-start | bytes 1216512 | tf_op jit(solution)/shard_map/all_gather | solution.py:236
  12.7 544.6 %all-gather.26.cloned.1.call-start = ((), (), s32[]{:S(2)}) async-start(), calls=%async_computation.20 | async-start | bytes 3649536 | tf_op jit(solution)/shard_map/all_gather | solution.py:237
  13.4 599.5 %all-gather.28.cloned.1.call-start = ((), (), s32[]{:S(2)}) async-start(), calls=%async_computation.21 | async-start | bytes 1216512 | tf_op jit(solution)/shard_map/all_gather | solution.py:238
  14.0 664.3 %all-gather.30.cloned.1.call-start = ((), (), s32[]{:S(2)}) async-start(), calls=%async_computation.22 | async-start | bytes 4866048 | tf_op jit(solution)/shard_map/all_gather | solution.py:239
  14.7 728.7 %all-gather.32.cloned.1.call-start = ((), (), s32[]{:S(2)}) async-start(), calls=%async_computation.23 | async-start | bytes 4866048 | tf_op jit(solution)/shard_map/all_gather | solution.py:240
  15.3 816.2 %reduce-scatter.44.cloned.1.call-start = ((), (), s32[]{:S(2)}) async-start(), calls=%async_computation.38 | async-start | bytes 245760 | tf_op jit(solution)/shard_map/reduce_scatter | solution.py:316
  94.3 218.2 %copy-start.136 = (f32[768]{0:T(1024)}, f32[768]{0:T(1024)S(1)}, u32[]{:S(2)}) copy-start(f32[768]{0:T(1024)S(1)} %get-tuple-element.43) | copy-start | bytes 9220
  94.3 345.2 %copy-start.99 = (f32[768]{0:T(1024)}, f32[768]{0:T(1024)S(1)}, u32[]{:S(2)}) copy-start(f32[768]{0:T(1024)S(1)} %get-tuple-element.38) | copy-start | bytes 9220
  94.3 351.7 %copy-start.97 = (f32[768]{0:T(1024)}, f32[768]{0:T(1024)S(1)}, u32[]{:S(2)}) copy-start(f32[768]{0:T(1024)S(1)} %get-tuple-element.42) | copy-start | bytes 9220
  94.3 404.3 %copy-start.91 = (f32[768]{0:T(1024)}, f32[768]{0:T(1024)S(1)}, u32[]{:S(2)}) copy-start(f32[768]{0:T(1024)S(1)} %get-tuple-element.40) | copy-start | bytes 9220
  131.7 326.1 %copy-start.73 = (bf16[4,8,12,64]{3,2,1,0:T(8,128)(2,1)}, bf16[4,8,12,64]{3,2,1,0:T(8,128)(2,1)S(1)}, u32[]{:S(2)}) copy-start(bf16[4,8,12,64]{3,2,1,0:T(8,128)(2,1)S(1)} %reshape.720) | copy-start | bytes 147460
  390.1 544.6 %copy-start.4 = (f32[4,256,768]{2,1,0:T(8,128)}, f32[4,256,768]{2,1,0:T(8,128)S(1)}, u32[]{:S(2)}) copy-start(f32[4,256,768]{2,1,0:T(8,128)S(1)} %get-tuple-element.76) | copy-start | bytes 9437188
  796.4 50.2 %reduce-scatter.46.cloned.1.call-start = ((), (), s32[]{:S(2)}) async-start(), calls=%async_computation.39 | async-start | bytes 245760 | tf_op jit(solution)/shard_map/reduce_scatter | solution.py:319
  802.2 300.9 %reduce-scatter.42.cloned.1.call-start = ((), (), s32[]{:S(2)}) async-start(), calls=%async_computation.37 | async-start | bytes 2433024 | tf_op jit(solution)/shard_map/reduce_scatter | solution.py:377
  808.4 294.7 %reduce-scatter.34.cloned.1.call-start = ((), (), s32[]{:S(2)}) async-start(), calls=%async_computation.33 | async-start | bytes 2433024 | tf_op jit(solution)/shard_map/reduce_scatter | solution.py:373
  829.1 330.7 %reduce-scatter.22.cloned.1.call-start = ((), (), s32[]{:S(2)}) async-start(), calls=%async_computation.27 | async-start | bytes 2433024 | tf_op jit(solution)/shard_map/reduce_scatter | solution.py:367
  919.1 345.4 %reduce-scatter.30.cloned.1.call-start = ((), (), s32[]{:S(2)}) async-start(), calls=%async_computation.31 | async-start | bytes 2433024 | tf_op jit(solution)/shard_map/reduce_scatter | solution.py:371
  924.2 464.8 %reduce-scatter.40.cloned.1.call-start = ((), (), s32[]{:S(2)}) async-start(), calls=%async_computation.36 | async-start | bytes 7299072 | tf_op jit(solution)/shard_map/reduce_scatter | solution.py:376
  931.1 583.1 %reduce-scatter.28.cloned.1.call-start = ((), (), s32[]{:S(2)}) async-start(), calls=%async_computation.30 | async-start | bytes 7299072 | tf_op jit(solution)/shard_map/reduce_scatter | solution.py:370
  942.5 696.6 %reduce-scatter.32.cloned.1.call-start = ((), (), s32[]{:S(2)}) async-start(), calls=%async_computation.32 | async-start | bytes 7299072 | tf_op jit(solution)/shard_map/reduce_scatter | solution.py:372
  948.1 816.6 %reduce-scatter.20.cloned.1.call-start = ((), (), s32[]{:S(2)}) async-start(), calls=%async_computation.26 | async-start | bytes 7299072 | tf_op jit(solution)/shard_map/reduce_scatter | solution.py:366
  1002.9 903.3 %reduce-scatter.38.cloned.1.call-start = ((), (), s32[]{:S(2)}) async-start(), calls=%async_computation.35 | async-start | bytes 9732096 | tf_op jit(solution)/shard_map/reduce_scatter | solution.py:375
  1009.7 1038.4 %reduce-scatter.36.cloned.1.call-start = ((), (), s32[]{:S(2)}) async-start(), calls=%async_computation.34 | async-start | bytes 9732096 | tf_op jit(solution)/shard_map/reduce_scatter | solution.py:374
  1015.7 1173.4 %reduce-scatter.24.cloned.1.call-start = ((), (), s32[]{:S(2)}) async-start(), calls=%async_computation.28 | async-start | bytes 9732096 | tf_op jit(solution)/shard_map/reduce_scatter | solution.py:368
  1027.2 1303.8 %reduce-scatter.26.cloned.1.call-start = ((), (), s32[]{:S(2)}) async-start(), calls=%async_computation.29 | async-start | bytes 9732096 | tf_op jit(solution)/shard_map/reduce_scatter | solution.py:369
  (170 other events, 2645.3 us)
Sparse Core Ops, SparseCore 0:
  10.9 56.7 all-gather.35
  70.6 59.1 all-gather.21
  132.7 58.8 all-gather.13
  194.4 52.8 all-gather.15
  250.0 62.4 all-gather.17
  315.3 62.3 all-gather.19
  380.5 58.9 all-gather.33
  442.4 52.8 all-gather.23
  498.2 59.0 all-gather.25
  560.0 52.8 all-gather.27
  615.8 62.4 all-gather.29
  681.1 62.3 all-gather.31
  796.5 22.8 reduce-scatter.43
  822.5 23.9 reduce-scatter.45
  852.3 99.0 reduce-scatter.41
  958.0 98.0 reduce-scatter.33
  1061.8 98.0 reduce-scatter.21
  1166.4 98.0 reduce-scatter.29
  1270.8 118.1 reduce-scatter.39
  1396.0 118.2 reduce-scatter.27
  1520.5 118.5 reduce-scatter.31
  1646.3 118.3 reduce-scatter.19
  1771.2 134.9 reduce-scatter.37
  1913.5 134.5 reduce-scatter.35
  2054.5 134.6 reduce-scatter.23
  2196.5 134.4 reduce-scatter.25
where the time goes:
time: 2350 us; the launch traced here: 2340 us
  waiting for transfers between devices  1770 us (75%)
  matrix products  268 us (11%)
  blocking collectives  120 us (5%)
  local copies, waits for them, and re-layouts  94.4 us (4%)
  other arithmetic  65.7 us (3%)
    reduce_scatter x1, waiting for transfers between devices, shards(): lax.psum_scatter(latent_up_grad, ('dp', 'fsdp'), scatter_dimension=0, til...  142 us
    reduce_scatter x1, waiting for transfers between devices, shards(): lax.psum_scatter(token_down_grad, ('dp', 'fsdp'), scatter_dimension=0, ti...  142 us
    reduce_scatter x1, waiting for transfers between devices, shards(): lax.psum_scatter(latent_down_grad, ('dp', 'fsdp'), scatter_dimension=0, t...  141 us
    reduce_scatter x1, waiting for transfers between devices, shards(): lax.psum_scatter(token_up_grad, ('dp', 'fsdp'), scatter_dimension=0, tile...  141 us
    reduce_scatter x1, waiting for transfers between devices, shards(): lax.psum_scatter(local_qkv_grad, ('dp', 'fsdp'), scatter_dimension=0, til...  126 us
    reduce_scatter x1, waiting for transfers between devices, shards(): lax.psum_scatter(read_qkv_grad, ('dp', 'fsdp'), scatter_dimension=0, tile...  125 us
    reduce_scatter x1, waiting for transfers between devices, shards(): lax.psum_scatter(global_qkv_grad, ('dp', 'fsdp'), scatter_dimension=0, ti...  125 us
    reduce_scatter x1, waiting for transfers between devices, shards(): lax.psum_scatter(write_qkv_grad, ('dp', 'fsdp'), scatter_dimension=0, til...  124 us
  transfers between devices with their start and end apart: 26, of which 22 were waited for; matrix products, arithmetic and copies ran while one was open for 15% of the time, Pallas kernels for 0%

commit v1 on v0

--- a/solution.py
+++ b/solution.py
@@ -1,6 +1,9 @@
+import functools
 import jax
 import jax.numpy as jnp
 from jax import lax
+from jax.experimental import pallas as pl
+from jax.experimental.pallas import tpu as pltpu
 from jax.sharding import PartitionSpec as P
 
 HDIM = 64
@@ -86,10 +89,6 @@
     probs_low = probs_full.astype(jnp.bfloat16)
     value_heads = split_heads(value_bf)
     grad_heads = split_heads(grad_mixed)
-    mixed = jnp.einsum(
-        "bhqk,bkhe->bqhe", probs_low, value_heads, preferred_element_type=jnp.float32
-    )
-    mixed = mixed.reshape(query_bf.shape).astype(jnp.bfloat16)
     grad_probs = jnp.einsum(
         "bqhe,bkhe->bhqk", grad_heads, value_heads, preferred_element_type=jnp.float32
     )
@@ -117,7 +116,6 @@
         "bhqk,bqhe->bkhe", probs_low, grad_heads, preferred_element_type=jnp.float32
     )
     return (
-        mixed,
         grad_query.reshape(query_bf.shape),
         grad_key.reshape(key_bf.shape),
         grad_value.reshape(value_bf.shape),
@@ -137,17 +135,17 @@
     mixed, log_total = attend(
         query_bf, key_values[..., :model_width], key_values[..., model_width:], key_bias
     )
-    return (project(mixed, out_weight), log_total)
+    return (project(mixed, out_weight), (query_bf, key_values, mixed, log_total))
 
 
 def block_attention_back(
-    query_norm, key_norm, qkv_weight, out_weight, key_bias, log_total, grad_branch
+    query_norm, key_norm, qkv_weight, out_weight, key_bias, kept, grad_branch
 ):
     model_width = query_norm.shape[-1]
-    query_bf, key_values = queries_keys(query_norm, key_norm, qkv_weight)
+    query_bf, key_values, mixed, log_total = kept
     branch_bf = grad_branch.astype(jnp.bfloat16)
     grad_mixed = back_project(branch_bf, out_weight).astype(jnp.bfloat16)
-    mixed, grad_query, grad_key, grad_value = attend_back(
+    grad_query, grad_key, grad_value = attend_back(
         query_bf,
         key_values[..., :model_width],
         key_values[..., model_width:],
@@ -169,21 +167,341 @@
 def mlp_forward(norm_rows, up_weight, down_weight):
     hidden_pre = project(norm_rows, up_weight)
     activated = gelu_tanh(hidden_pre).astype(jnp.bfloat16)
-    return project(activated, down_weight)
-
-
-def mlp_back(norm_rows, up_weight, down_weight, grad_branch):
+    return (project(activated, down_weight), activated)
+
+
+def mlp_back(norm_rows, up_weight, down_weight, act_bf, grad_branch):
     hidden_pre = project(norm_rows, up_weight)
-    activated, pullback = jax.vjp(gelu_tanh, hidden_pre)
-    act_bf = activated.astype(jnp.bfloat16)
+    _, pullback = jax.vjp(gelu_tanh, hidden_pre)
     branch_bf = grad_branch.astype(jnp.bfloat16)
     grad_act = back_project(branch_bf, down_weight)
     grad_pre = pullback(grad_act)[0].astype(jnp.bfloat16)
+    model_width = branch_bf.shape[-1]
+    pieces = act_bf.shape[-1] // model_width
     return (
         back_project(grad_pre, up_weight),
         weight_grad(grad_pre, norm_rows),
-        weight_grad(branch_bf, act_bf),
-    )
+        [
+            weight_grad(branch_bf, act_bf[..., model_width * j : model_width * (j + 1)])
+            for j in range(pieces)
+        ],
+    )
+
+
+MESH_ID = pl.DeviceIdType.MESH
+ALL_AXES = ("dp", "fsdp")
+
+
+def place():
+    dp_index = lax.axis_index("dp")
+    fsdp_index = lax.axis_index("fsdp")
+    return (dp_index // 2, dp_index % 2, fsdp_index // 2, fsdp_index % 2)
+
+
+def device(z, core, y, x):
+    return {"dp": z * 2 + core, "fsdp": y * 2 + x}
+
+
+def remote(src, dst, send_sem, recv_sem, target):
+    return pltpu.make_async_remote_copy(
+        src, dst, send_sem, recv_sem, device_id=target, device_id_type=MESH_ID
+    )
+
+
+def greet(peers):
+    barrier = pltpu.get_barrier_semaphore()
+    for peer in peers:
+        pl.semaphore_signal(barrier, inc=1, device_id=peer, device_id_type=MESH_ID)
+    pl.semaphore_wait(barrier, len(peers))
+
+
+def scatter_kernel(groups, count, *refs):
+    chunks = len(groups)
+    ins = refs[:count]
+    outs = refs[count : count + chunks]
+    own, pair, first_b, first_c, second_b, second_c, last = refs[count + chunks : count + chunks + 7]
+    local_sem, s0, q0, s1, q1, s2, q2, s3, q3 = refs[count + chunks + 7 :]
+    z, core, y, x = place()
+    half = ins[0].shape[-1] // 2
+    sibling = device(z, 1 - core, y, x)
+    over_x = device(z, core, y, 1 - x)
+    over_y = device(z, core, 1 - y, x)
+    over_z = [device((z + step) % 4, core, y, x) for step in (1, 2, 3)]
+    greet([sibling, over_x, over_y] + over_z)
+    f32 = jnp.float32
+    bf16 = jnp.bfloat16
+    left = pl.ds(0, half)
+    right = pl.ds(half, half)
+    rows_of = [sum(rows for _, rows in group) for group in groups]
+
+    def copies_pair(k):
+        made = []
+        offset = 0
+        for j, (i, rows) in enumerate(groups[k]):
+            spot = pl.ds(offset, rows)
+            made.append(
+                (
+                    pltpu.make_async_copy(
+                        ins[i].at[:, core], own.at[k, :, :, :, spot, :], local_sem.at[k, j]
+                    ),
+                    remote(
+                        ins[i].at[:, 1 - core],
+                        pair.at[k, :, :, :, spot, :],
+                        s0.at[k, j],
+                        q0.at[k, j],
+                        sibling,
+                    ),
+                )
+            )
+            offset += rows
+        return made
+
+    def copies_first(k):
+        spot = pl.ds(0, rows_of[k])
+        return [
+            remote(
+                own.at[k, :, 1 - y, :, spot, left],
+                first_b.at[k, :, :, spot],
+                s1.at[k, 0],
+                q1.at[k, 0],
+                over_y,
+            ),
+            remote(
+                own.at[k, :, :, 1 - x, spot, right],
+                first_c.at[k, :, :, spot],
+                s1.at[k, 1],
+                q1.at[k, 1],
+                over_x,
+            ),
+        ]
+
+    def copies_second(k):
+        spot = pl.ds(0, rows_of[k])
+        return [
+            remote(
+                first_b.at[k, :, 1 - x, spot],
+                second_b.at[k, :, spot],
+                s2.at[k, 0],
+                q2.at[k, 0],
+                over_x,
+            ),
+            remote(
+                first_c.at[k, :, 1 - y, spot],
+                second_c.at[k, :, spot],
+                s2.at[k, 1],
+                q2.at[k, 1],
+                over_y,
+            ),
+        ]
+
+    def copies_last(k):
+        spot = pl.ds(0, rows_of[k])
+        made = []
+        for step in (1, 2, 3):
+            goal = (z + step) % 4
+            for side, (source, place_at) in enumerate(((second_b, left), (second_c, right))):
+                made.append(
+                    remote(
+                        source.at[k, goal, spot],
+                        last.at[k, step - 1, spot, place_at],
+                        s3.at[k, step - 1, side],
+                        q3.at[k, step - 1, side],
+                        over_z[step - 1],
+                    )
+                )
+        return made
+
+    pairs = [copies_pair(k) for k in range(chunks)]
+    firsts = [copies_first(k) for k in range(chunks)]
+    seconds = [copies_second(k) for k in range(chunks)]
+    lasts = [copies_last(k) for k in range(chunks)]
+
+    def start_pair(k):
+        for local, far in pairs[k]:
+            local.start()
+            far.start()
+
+    def stage_pair(k):
+        rows = rows_of[k]
+        for local, far in pairs[k]:
+            local.wait()
+            far.wait_recv()
+        if k + 2 < chunks:
+            start_pair(k + 2)
+
+        def step(i, carry):
+            zz, yy, xx = i // 4, (i // 2) % 2, i % 2
+            own[k, zz, yy, xx, :rows] = (
+                own[k, zz, yy, xx, :rows].astype(f32) + pair[k, zz, yy, xx, :rows].astype(f32)
+            ).astype(bf16)
+            return carry
+
+        lax.fori_loop(0, 16, step, 0)
+        for copy in firsts[k]:
+            copy.start()
+
+    def stage_first(k):
+        rows = rows_of[k]
+        for copy in firsts[k]:
+            copy.wait_recv()
+
+        def step(i, carry):
+            zz, other = i // 2, i % 2
+            first_b[k, zz, other, :rows] = (
+                own[k, zz, y, other, :rows, :half].astype(f32)
+                + first_b[k, zz, other, :rows].astype(f32)
+            ).astype(bf16)
+            first_c[k, zz, other, :rows] = (
+                own[k, zz, other, x, :rows, half:].astype(f32)
+                + first_c[k, zz, other, :rows].astype(f32)
+            ).astype(bf16)
+            return carry
+
+        lax.fori_loop(0, 8, step, 0)
+        for copy in seconds[k]:
+            copy.start()
+
+    def stage_second(k):
+        rows = rows_of[k]
+        for copy in seconds[k]:
+            copy.wait_recv()
+
+        def step(zz, carry):
+            second_b[k, zz, :rows] = (
+                first_b[k, zz, x, :rows].astype(f32) + second_b[k, zz, :rows].astype(f32)
+            ).astype(bf16)
+            second_c[k, zz, :rows] = (
+                first_c[k, zz, y, :rows].astype(f32) + second_c[k, zz, :rows].astype(f32)
+            ).astype(bf16)
+            return carry
+
+        lax.fori_loop(0, 4, step, 0)
+        for copy in lasts[k]:
+            copy.start()
+
+    def stage_last(k):
+        rows = rows_of[k]
+        for copy in lasts[k]:
+            copy.wait_recv()
+        for source, low in ((second_b, 0), (second_c, half)):
+            total = source[k, z, :rows].astype(f32)
+            for step in range(3):
+                total = total + last[k, step, :rows, low : low + half].astype(f32)
+            outs[k][:, low : low + half] = total
+
+    start_pair(0)
+    if chunks > 1:
+        start_pair(1)
+    for turn in range(chunks + 3):
+        if turn < chunks:
+            stage_pair(turn)
+        if 0 <= turn - 1 < chunks:
+            stage_first(turn - 1)
+        if 0 <= turn - 2 < chunks:
+            stage_second(turn - 2)
+        if 0 <= turn - 3 < chunks:
+            stage_last(turn - 3)
+    for k in range(chunks):
+        for _, far in pairs[k]:
+            far.wait_send()
+        for copy in firsts[k] + seconds[k] + lasts[k]:
+            copy.wait_send()
+
+
+def scatter_sums(arrays, groups, call_id):
+    cols = arrays[0].shape[1]
+    half = cols // 2
+    chunks = len(groups)
+    rows_of = [sum(rows for _, rows in group) for group in groups]
+    most = max(rows_of)
+    parts = max(len(group) for group in groups)
+    ins = [array.reshape(4, 2, 2, 2, array.shape[0] // 32, cols) for array in arrays]
+    bf16 = jnp.bfloat16
+    vmem = pltpu.VMEM
+    dma = pltpu.SemaphoreType.DMA
+    return pl.pallas_call(
+        functools.partial(scatter_kernel, groups, len(ins)),
+        out_shape=[jax.ShapeDtypeStruct((rows, cols), jnp.float32) for rows in rows_of],
+        in_specs=[pl.BlockSpec(memory_space=pl.ANY)] * len(ins),
+        out_specs=[pl.BlockSpec(memory_space=pltpu.VMEM)] * chunks,
+        scratch_shapes=[
+            vmem((chunks, 4, 2, 2, most, cols), bf16),
+            vmem((chunks, 4, 2, 2, most, cols), bf16),
+            vmem((chunks, 4, 2, most, half), bf16),
+            vmem((chunks, 4, 2, most, half), bf16),
+            vmem((chunks, 4, most, half), bf16),
+            vmem((chunks, 4, most, half), bf16),
+            vmem((chunks, 3, most, cols), bf16),
+            dma((chunks, parts)),
+            dma((chunks, parts)),
+            dma((chunks, parts)),
+            dma((chunks, 2)),
+            dma((chunks, 2)),
+            dma((chunks, 2)),
+            dma((chunks, 2)),
+            dma((chunks, 3, 2)),
+            dma((chunks, 3, 2)),
+        ],
+        compiler_params=pltpu.CompilerParams(
+            collective_id=call_id, has_side_effects=True, vmem_limit_bytes=66 * 1024 * 1024
+        ),
+        name="scatter_sums",
+    )(*ins)
+
+
+def fold_columns(shard):
+    rows, cols = shard.shape
+    width = 768 if cols % 768 == 0 else cols
+    return shard.reshape(rows, cols // width, width).transpose(1, 0, 2).reshape(-1, width)
+
+
+def unfold_columns(folded, devices):
+    width = folded.shape[1]
+    rows = width // devices
+    pieces = folded.shape[0] // width
+    split = folded.reshape(devices, pieces, rows, width).transpose(0, 2, 1, 3)
+    return split.reshape(width, pieces * width)
+
+
+def gather_packed(shards_in, devices):
+    packed = jnp.concatenate(shards_in, axis=0)
+    gathered = lax.all_gather(packed, ALL_AXES, axis=0)
+    found = []
+    offset = 0
+    for shard in shards_in:
+        rows = shard.shape[0]
+        found.append(gathered[:, offset : offset + rows].reshape(devices * rows, shard.shape[1]))
+        offset += rows
+    return found
+
+
+def reduce_grads(groups, devices):
+    arrays = []
+    chunks = []
+    for group in groups:
+        chunk = []
+        for array in group:
+            chunk.append((len(arrays), array.shape[0] // devices))
+            arrays.append(array.astype(jnp.bfloat16))
+        chunks.append(chunk)
+    if (lax.axis_size("dp"), lax.axis_size("fsdp")) == (8, 4):
+        sums = scatter_sums(arrays, chunks, 1)
+        found = []
+        for total, chunk in zip(sums, chunks):
+            offset = 0
+            parts = []
+            for _, rows in chunk:
+                parts.append(total[offset : offset + rows])
+                offset += rows
+            found.append(parts)
+        return found
+    return [
+        [
+            lax.psum_scatter(array.astype(jnp.float32), ALL_AXES, scatter_dimension=0, tiled=True)
+            for array in group
+        ]
+        for group in groups
+    ]
 
 
 def shards(
@@ -224,36 +542,43 @@
         jnp.float32
     )[None]
     empty_bias = jnp.zeros((group_count, 1, LAT), jnp.float32)
-    token_side = (
-        lax.all_gather(local_qkv, ("dp", "fsdp"), axis=0, tiled=True),
-        lax.all_gather(local_out, ("dp", "fsdp"), axis=0, tiled=True),
-        lax.all_gather(token_up, ("dp", "fsdp"), axis=0, tiled=True),
-        lax.all_gather(token_down, ("dp", "fsdp"), axis=0, tiled=True),
-        lax.all_gather(norm_gains, ("dp", "fsdp"), axis=1, tiled=True),
-    )
-    latent_side = (
-        lax.all_gather(read_qkv, ("dp", "fsdp"), axis=0, tiled=True),
-        lax.all_gather(read_out, ("dp", "fsdp"), axis=0, tiled=True),
-        lax.all_gather(global_qkv, ("dp", "fsdp"), axis=0, tiled=True),
-        lax.all_gather(global_out, ("dp", "fsdp"), axis=0, tiled=True),
-        lax.all_gather(latent_up, ("dp", "fsdp"), axis=0, tiled=True),
-        lax.all_gather(latent_down, ("dp", "fsdp"), axis=0, tiled=True),
-        lax.all_gather(write_qkv, ("dp", "fsdp"), axis=0, tiled=True),
-        lax.all_gather(write_out, ("dp", "fsdp"), axis=0, tiled=True),
-    )
-    gain_rows = token_side[4].astype(jnp.float32)
+    devices = lax.axis_size("dp") * lax.axis_size("fsdp")
+    gain_part = norm_gains.reshape(1, -1)
+    gain_part = jnp.pad(gain_part, ((0, 7), (0, model_width - gain_part.shape[1])))
+    weights = gather_packed(
+        [local_qkv, local_out, token_up, fold_columns(token_down), gain_part], devices
+    )
+    token_side = (weights[0], weights[1], weights[2], unfold_columns(weights[3], devices))
+    gain_all = weights[4].reshape(devices, 8, model_width)[:, 0, : norm_gains.size]
+    gain_all = gain_all.reshape(devices, 8, norm_gains.shape[1]).transpose(1, 0, 2)
+    gain_rows = gain_all.reshape(8, model_width).astype(jnp.float32)
+    weights = gather_packed(
+        [
+            read_qkv,
+            read_out,
+            global_qkv,
+            global_out,
+            latent_up,
+            fold_columns(latent_down),
+            write_qkv,
+            write_out,
+        ],
+        devices,
+    )
+    latent_side = tuple(weights[:5]) + (unfold_columns(weights[5], devices),) + tuple(weights[6:])
     residual_in = tokens.astype(jnp.float32).reshape(group_count, GROUP, model_width)
     local_norm = layer_norm(residual_in, gain_rows[0]).astype(jnp.bfloat16)
-    branch, local_total = block_attention(
+    branch, local_kept = block_attention(
         local_norm, local_norm, token_side[0], token_side[1], token_bias
     )
     residual_one = residual_in + branch
     token_norm = layer_norm(residual_one, gain_rows[1]).astype(jnp.bfloat16)
-    residual_two = residual_one + mlp_forward(token_norm, token_side[2], token_side[3])
+    branch, token_act = mlp_forward(token_norm, token_side[2], token_side[3])
+    residual_two = residual_one + branch
     latent_in = latents.astype(jnp.float32).reshape(group_count, LAT, model_width)
     read_query = layer_norm(latent_in, gain_rows[2]).astype(jnp.bfloat16)
     read_keys = layer_norm(residual_two, gain_rows[3]).astype(jnp.bfloat16)
-    branch, read_total = block_attention(
+    branch, read_kept = block_attention(
         read_query, read_keys, latent_side[0], latent_side[1], token_bias
     )
     latent_one = (latent_in + branch).reshape(latent_count, model_width)
@@ -268,11 +593,12 @@
     )
     latent_two = latent_one + project(global_mixed[0], latent_side[3])
     latent_norm = layer_norm(latent_two, gain_rows[5]).astype(jnp.bfloat16)
-    latent_out = latent_two + mlp_forward(latent_norm, latent_side[4], latent_side[5])
+    branch, latent_act = mlp_forward(latent_norm, latent_side[4], latent_side[5])
+    latent_out = latent_two + branch
     latent_groups = latent_out.reshape(group_count, LAT, model_width)
     write_query = layer_norm(residual_two, gain_rows[6]).astype(jnp.bfloat16)
     write_keys = layer_norm(latent_groups, gain_rows[7]).astype(jnp.bfloat16)
-    branch, write_total = block_attention(
+    branch, write_kept = block_attention(
         write_query, write_keys, latent_side[6], latent_side[7], empty_bias
     )
     residual_out = residual_two + branch
@@ -290,7 +616,7 @@
         back_all[10],
         back_all[11],
         empty_bias,
-        write_total,
+        write_kept,
         grad_residual_out,
     )
     grad_values, grad_gain_six = norm_back(residual_two, gain_rows[6], grad_query_norm)
@@ -298,13 +624,13 @@
     grad_values, grad_gain_seven = norm_back(latent_groups, gain_rows[7], grad_key_norm)
     grad_latent_out = grad_latent_out + grad_values.reshape(latent_count, model_width)
     grad_norm_rows, latent_up_grad, latent_down_grad = mlp_back(
-        latent_norm, back_all[8], back_all[9], grad_latent_out
+        latent_norm, back_all[8], back_all[9], latent_act, grad_latent_out
     )
     grad_values, grad_gain_five = norm_back(latent_two, gain_rows[5], grad_norm_rows)
     grad_latent_two = grad_latent_out + grad_values
     branch_bf = grad_latent_two.astype(jnp.bfloat16)
     grad_mixed = back_project(branch_bf, back_all[7]).astype(jnp.bfloat16)
-    mixed_again, grad_query, grad_key, grad_value = attend_back(
+    grad_query, grad_key, grad_value = attend_back(
         global_query[None],
         gathered[None, :, :model_width],
         gathered[None, :, model_width:],
@@ -312,39 +638,37 @@
         global_total,
         grad_mixed[None],
     )
-    own_key, own_value = (
-        lax.psum_scatter(
-            grad_key[0].astype(jnp.bfloat16), "fsdp", scatter_dimension=0, tiled=True
-        ).astype(jnp.float32),
-        lax.psum_scatter(
-            grad_value[0].astype(jnp.bfloat16), "fsdp", scatter_dimension=0, tiled=True
-        ).astype(jnp.float32),
+    own_both = lax.psum_scatter(
+        jnp.concatenate([grad_key[0], grad_value[0]], axis=-1).astype(jnp.bfloat16),
+        "fsdp",
+        scatter_dimension=0,
+        tiled=True,
     )
     query_grad_bf = grad_query[0].astype(jnp.bfloat16)
-    keyval_grad_bf = jnp.concatenate([own_key, own_value], axis=-1).astype(jnp.bfloat16)
+    keyval_grad_bf = own_both.astype(jnp.bfloat16)
     global_qkv_grad = jnp.concatenate(
         [weight_grad(query_grad_bf, global_norm), weight_grad(keyval_grad_bf, global_norm)], axis=0
     )
-    global_out_grad = weight_grad(branch_bf, mixed_again[0])
+    global_out_grad = weight_grad(branch_bf, global_mixed[0])
     grad_norm_rows = back_project(query_grad_bf, back_all[6][:model_width]) + back_project(
         keyval_grad_bf, back_all[6][model_width:]
     )
     grad_values, grad_gain_four = norm_back(latent_one, gain_rows[4], grad_norm_rows)
     grad_latent_one = (grad_latent_two + grad_values).reshape(group_count, LAT, model_width)
     grad_query_norm, grad_key_norm, read_qkv_grad, read_out_grad = block_attention_back(
-        read_query, read_keys, back_all[4], back_all[5], token_bias, read_total, grad_latent_one
+        read_query, read_keys, back_all[4], back_all[5], token_bias, read_kept, grad_latent_one
     )
     grad_values, grad_gain_two = norm_back(latent_in, gain_rows[2], grad_query_norm)
     grad_latent_in = grad_latent_one + grad_values
     grad_values, grad_gain_three = norm_back(residual_two, gain_rows[3], grad_key_norm)
     grad_residual_two = grad_residual_two + grad_values
     grad_norm_rows, token_up_grad, token_down_grad = mlp_back(
-        token_norm, back_all[2], back_all[3], grad_residual_two
+        token_norm, back_all[2], back_all[3], token_act, grad_residual_two
     )
     grad_values, grad_gain_one = norm_back(residual_one, gain_rows[1], grad_norm_rows)
     grad_residual_one = grad_residual_two + grad_values
     grad_query_norm, grad_key_norm, local_qkv_grad, local_out_grad = block_attention_back(
-        local_norm, local_norm, back_all[0], back_all[1], token_bias, local_total, grad_residual_one
+        local_norm, local_norm, back_all[0], back_all[1], token_bias, local_kept, grad_residual_one
     )
     grad_values, grad_gain_zero = norm_back(
         residual_in, gain_rows[0], grad_query_norm + grad_key_norm
@@ -362,41 +686,42 @@
             grad_gain_seven,
         ]
     )
-    summed = (
-        lax.psum_scatter(local_qkv_grad, ("dp", "fsdp"), scatter_dimension=0, tiled=True),
-        lax.psum_scatter(local_out_grad, ("dp", "fsdp"), scatter_dimension=0, tiled=True),
-        lax.psum_scatter(token_up_grad, ("dp", "fsdp"), scatter_dimension=0, tiled=True),
-        lax.psum_scatter(token_down_grad, ("dp", "fsdp"), scatter_dimension=0, tiled=True),
-        lax.psum_scatter(read_qkv_grad, ("dp", "fsdp"), scatter_dimension=0, tiled=True),
-        lax.psum_scatter(read_out_grad, ("dp", "fsdp"), scatter_dimension=0, tiled=True),
-        lax.psum_scatter(global_qkv_grad, ("dp", "fsdp"), scatter_dimension=0, tiled=True),
-        lax.psum_scatter(global_out_grad, ("dp", "fsdp"), scatter_dimension=0, tiled=True),
-        lax.psum_scatter(latent_up_grad, ("dp", "fsdp"), scatter_dimension=0, tiled=True),
-        lax.psum_scatter(latent_down_grad, ("dp", "fsdp"), scatter_dimension=0, tiled=True),
-        lax.psum_scatter(write_qkv_grad, ("dp", "fsdp"), scatter_dimension=0, tiled=True),
-        lax.psum_scatter(write_out_grad, ("dp", "fsdp"), scatter_dimension=0, tiled=True),
-        lax.psum_scatter(gain_grads, ("dp", "fsdp"), scatter_dimension=1, tiled=True),
-    )
-    weight_sums = tuple(summed[:12])
-    gain_sum = summed[12]
+    gain_cols = norm_gains.shape[1]
+    gain_split = gain_grads.reshape(8, devices, gain_cols).transpose(1, 0, 2)
+    gain_split = gain_split.reshape(devices, 1, 8 * gain_cols)
+    gain_split = jnp.pad(gain_split, ((0, 0), (0, 7), (0, model_width - 8 * gain_cols)))
+    sums = reduce_grads(
+        [
+            [write_qkv_grad, write_out_grad],
+            [latent_up_grad],
+            latent_down_grad,
+            [global_qkv_grad, global_out_grad],
+            [read_qkv_grad, read_out_grad],
+            [token_up_grad],
+            token_down_grad,
+            [local_qkv_grad, local_out_grad, gain_split.reshape(-1, model_width)],
+        ],
+        devices,
+    )
+    gain_sum = sums[7][2][0, : 8 * gain_cols].reshape(8, gain_cols)
     return (
         out_tokens,
         out_latents,
         grad_residual_in.reshape(-1, model_width),
         grad_latent_in.reshape(-1, model_width),
         gain_sum,
-        weight_sums[0],
-        weight_sums[1],
-        weight_sums[2],
-        weight_sums[3],
-        weight_sums[4],
-        weight_sums[5],
-        weight_sums[6],
-        weight_sums[7],
-        weight_sums[8],
-        weight_sums[9],
-        weight_sums[10],
-        weight_sums[11],
+        sums[7][0],
+        sums[7][1],
+        sums[5][0],
+        jnp.concatenate(sums[6], axis=1),
+        sums[4][0],
+        sums[4][1],
+        sums[3][0],
+        sums[3][1],
+        sums[1][0],
+        jnp.concatenate(sums[2], axis=1),
+        sums[0][0],
+        sums[0][1],
     )
 
 

time: 2350 us -> 835 us (0.36)
  waiting for transfers between devices: 1770 us -> 154 us
  Pallas kernels: 0 us -> 186 us
  blocking collectives: 120 us -> 9.64 us
  local copies, waits for them, and re-layouts: 94.4 us -> 162 us
  matrix products: 268 us -> 242 us
    reduce_scatter x14 -> x0, waiting for transfers between devices: 1240 us -> none  [the longest x1 142 us: shards(): lax.psum_scatter(latent_up_grad, ('dp', 'fsdp'), scatter_dimension=0, til...]
    all_gather x12 -> x2, waiting for transfers between devices: 523 us -> 151 us  [gather_packed(): gathered = lax.all_gather(packed, ALL_AXES, axis=0)]
    pallas_call x0 -> x1, Pallas kernels: none -> 186 us  [scatter_sums(): pl.pallas_call(functools.partial(scatter_kernel, groups, len(ins)), out_s...]
    all_gather x1 -> x0, blocking collectives: 70.3 us -> none  [shards(): lax.all_gather(norm_gains, ('dp', 'fsdp'), axis=1, tiled=True)]
    slice x0 -> x18, local copies, waits for them, and re-layouts: none -> 46.3 us  [the longest x6 31.9 us: gather_packed(): gathered[:, offset:offset + rows].reshape(devices * rows, shard.shape[1])]
    unnamed x1 -> x0, blocking collectives: 39.6 us -> none
    dot_general x16 -> x22, matrix products: 58.9 us -> 60.1 us  [weight_grad(): lax.dot_general(grad_flat, in_flat, (((0,), (0,)), ((), ())), preferred_e...]
  transfers between devices with their start and end apart: 26 -> 3, of which waited for: 22 -> 3; matrix products, arithmetic and copies ran while one was open for 15% -> 14% of each run, Pallas kernels for 0% -> 0%
where the time goes in v1:
time: 835 us; the launch traced here: 827 us
  matrix products  242 us (29%)
  Pallas kernels  186 us (22%)
  local copies, waits for them, and re-layouts  162 us (19%)
  waiting for transfers between devices  154 us (18%)
  other arithmetic  56.1 us (7%)
  between operations  16.4 us (2%)
  blocking collectives  9.64 us (1%)
    pallas_call x1, Pallas kernels, scatter_sums(): pl.pallas_call(functools.partial(scatter_kernel, groups, len(ins)), out_s...  186 us
    all_gather x2, waiting for transfers between devices, gather_packed(): gathered = lax.all_gather(packed, ALL_AXES, axis=0)  151 us
    dot_general x16, matrix products, back_project(): lax.dot_general(grad_rows, weight, (((grad_rows.ndim - 1,), (0,)), ((), (...  63.5 us
    dot_general x16, matrix products, project(): lax.dot_general(row_block, weight, (((row_block.ndim - 1,), (1,)), ((), (...  60.7 us
    dot_general x22, matrix products, weight_grad(): lax.dot_general(grad_flat, in_flat, (((0,), (0,)), ((), ())), preferred_e...  60.1 us
    unnamed x403, local copies, waits for them, and re-layouts  35.2 us
    slice x6, local copies, waits for them, and re-layouts, gather_packed(): gathered[:, offset:offset + rows].reshape(devices * rows, shard.shape[1])  31.9 us
  transfers between devices with their start and end apart: 3, of which 3 were waited for; matrix products, arithmetic and copies ran while one was open for 14% of the time, Pallas kernels for 0%

profile of v1, /device:TPU:0, one launch (start us, length us, event | category | flops | bytes accessed | tf_op | source)
XLA Modules:
  0.0 826.5 jit_solution(5191860547599212448)
XLA Ops:
  28.8 91.6 %all-gather.5.cloned.1.call-done = bf16[9472,768]{1,0:T(8,128)(2,1)} async-done(((bf16[296,768]{1,0:T(8,128)(2,1)}), bf16[9472,768]{1,0:T(8,128)(2,1)}) %all-gather.5.cloned.1.call-update) | async-done | bytes 14549008 | tf_op jit(solution)/shard_map/all_gather | solution.py:468
  123.7 4.0 slice.286
  130.7 6.7 fusion.156
  137.4 4.5 copy.328
  141.9 9.5 %reshape.933 = bf16[768,3072,1]{1,0,2:T(8,128)(2,1)} reshape(bf16[32,24,4,768]{3,2,1,0:T(4,128)(2,1)} %bitcast.374) | data formatting | bytes 9437184 | tf_op jit(solution)/shard_map/reshape | solution.py:463
  151.4 3.9 convolution_convert_fusion.11
  157.2 5.2 convolution_convert_fusion.2
  169.5 4.0 fusion.13
  185.7 11.0 %multiply_convert_fusion.1 = (bf16[4,256,3072]{2,1,0:T(8,128)(2,1)}, f32[4,256,3072]{2,1,0:T(8,128)}) fusion(bf16[3072,768,1]{1,0,2:T(8,128)(2,1)S(1)} %bitcast.429, f32[4,256,768]{2,1,0:T(8,128)S(1)} %get-tuple-element.110, f32[768]{0:T(1024)S(1)} %mul.727, f32[4,256]{1,0:T(4,128)S(1)} %fusion.134, f32[4,256]{1,0:T(4,128)S(1)} %broadcast_multiply_fusion.1), kind=kOutput, calls=%fused_computation.12 | convolution fusion | flops 4863295488 | bytes 26749952 | tf_op jit(solution)/shard_map/dot_general | solution.py:20
  196.7 8.4 %fusion.165 = (f32[4,256]{1,0:T(4,128)S(1)}, f32[4,256,768]{2,1,0:T(8,128)S(1)}) fusion(f32[4,256,768]{2,1,0:T(8,128)S(1)} %get-tuple-element.110, bf16[4,256,3072]{2,1,0:T(8,128)(2,1)} %get-tuple-element.111, bf16[768,3072,1]{1,0,2:T(8,128)(2,1)S(1)} %bitcast.424), kind=kOutput, calls=%fused_computation.388 | convolution fusion | flops 4833410048 | bytes 17305600 | tf_op jit(solution)/shard_map/dot_general | solution.py:20
  209.7 59.0 %all-gather.7.cloned.1.call-done = bf16[15360,768]{1,0:T(8,128)(2,1)} async-done(((bf16[480,768]{1,0:T(8,128)(2,1)}), bf16[15360,768]{1,0:T(8,128)(2,1)}) %all-gather.7.cloned.1.call-update) | async-done | bytes 23592976 | tf_op jit(solution)/shard_map/all_gather | solution.py:468
  272.5 7.9 fusion.154
  280.5 7.0 fusion.155
  290.0 4.7 convolution_convert_fusion.1
  320.7 4.7 copy.225
  335.9 9.6 %all_gather.19 = bf16[128,1536]{1,0:T(8,128)(2,1)S(1)} all-gather(bf16[32,1536]{1,0:T(8,128)(2,1)S(1)} %convolution_convert_fusion.5), channel_id=1, replica_groups=mesh['dp'=8,'fsdp'=4] {'fsdp'}, dimensions={0}, use_global_device_ids=true | all-gather | bytes 491520 | tf_op jit(solution)/shard_map/all_gather | solution.py:587
  355.5 4.6 multiply_convert_fusion.15
  425.6 4.5 bitcast_convert_fusion.12
  437.5 4.6 multiply_convert_fusion.8
  467.2 5.1 fusion.18
  472.4 4.5 bitcast_convert_fusion.2
  485.4 16.7 %fusion.6 = bf16[4,256,3072]{2,1,0:T(8,128)(2,1)} fusion(f32[4,256,3072]{2,1,0:T(8,128)} %get-tuple-element.112, bf16[4,256,768]{2,1,0:T(8,128)(2,1)S(1)} %get-tuple-element.63, bf16[768,3072,1]{1,0,2:T(8,128)(2,1)S(1)} %bitcast.426), kind=kOutput, calls=%fused_computation.8 | convolution fusion | flops 4894752768 | bytes 25165824 | tf_op jit(solution)/shard_map/dot_general | solution.py:29
  502.2 7.8 multiply_reduce_fusion.3
  510.0 7.9 bitcast_convert_fusion
  536.9 7.3 fusion.21
  544.2 10.0 %multiply_reduce_fusion = (f32[4,12,256]{2,1,0:T(8,128)S(1)}, f32[4,12,256,256]{2,3,1,0:T(8,128)}) fusion(f32[4,12,256]{2,1,0:T(8,128)S(1)} %copy-done.64, f32[4,256]{1,0:T(4,128)S(1)} %add.266, f32[4,12,256,256]{2,3,1,0:T(8,128)} %copy-done, bf16[4,256,12,64]{1,3,2,0:T(8,128)(2,1)S(1)} %bitcast.389, bf16[4,256,12,64]{1,3,2,0:T(8,128)(2,1)S(1)} %bitcast.416), kind=kOutput, calls=%fused_computation.10 | convolution fusion | flops 418369536 | bytes 28413952 | tf_op jit(solution)/shard_map/bqhe,bkhe->bhqk/dot_general | solution.py:92
  554.3 7.1 multiply_convert_fusion
  571.5 5.9 bitcast_convert_fusion.1
  577.4 4.3 fusion.17
  587.2 4.0 bitcast_convert_fusion.5
  608.1 185.8 %scatter_sums.1 = (f32[96,768]{1,0:T(8,128)}, f32[96,768]{1,0:T(8,128)}, f32[96,768]{1,0:T(8,128)}, f32[96,768]{1,0:T(8,128)}, f32[96,768]{1,0:T(8,128)}, /*inde...) custom-call(bf16[4,2,2,2,72,768]{5,4,3,2,1,0:T(8,128)(2,1)} %bitcast.378, ...), custom_call_target="tpu_custom_call" | custom-call | tf_op jit(solution)/shard_map/scatter_sums/pallas_call | solution.py:422
  810.5 5.7 add_add_fusion.4
  (647 shorter events, 282.7 us)
Async XLA Ops:
  7.2 15.4 %copy-start.121 = (bf16[24,768]{1,0:T(8,128)(2,1)S(1)}, bf16[24,768]{1,0:T(8,128)(2,1)}, u32[]{:S(2)}) copy-start(bf16[24,768]{1,0:T(8,128)(2,1)} %param.35) | copy-start | bytes 110596
  7.2 16.1 %copy-start.57 = (bf16[32,768]{1,0:T(8,128)(2,1)S(1)}, bf16[32,768]{1,0:T(8,128)(2,1)}, u32[]{:S(2)}) copy-start(bf16[32,768]{1,0:T(8,128)(2,1)} %param.19) | copy-start | bytes 147460
  7.2 17.8 %copy-start.150 = (s32[1024]{0:T(1024)S(1)}, s32[1024]{0:T(1024)}, u32[]{:S(2)}) copy-start(s32[1024]{0:T(1024)} %param.20) | copy-start | bytes 12292
  7.2 18.4 %copy-start.1 = (bf16[1024,768]{1,0:T(8,128)(2,1)S(1)}, bf16[1024,768]{1,0:T(8,128)(2,1)}, u32[]{:S(2)}) copy-start(bf16[1024,768]{1,0:T(8,128)(2,1)} %param.18) | copy-start | bytes 4718596
  7.2 113.2 %all-gather.5.cloned.1.call-start = ((), (), s32[]{:S(2)}) async-start(), calls=%async_computation.1 | async-start | bytes 15003648 | tf_op jit(solution)/shard_map/all_gather | solution.py:468
  12.7 256.0 %all-gather.7.cloned.1.call-start = ((), (), s32[]{:S(2)}) async-start(), calls=%async_computation.2 | async-start | bytes 24330240 | tf_op jit(solution)/shard_map/all_gather | solution.py:468
  23.2 421.8 %reduce-scatter.4.cloned.1.call-start = ((), (), s32[]{:S(2)}) async-start(), calls=%async_computation.3 | async-start | bytes 491520
  23.5 263.9 %copy-start.134 = (f32[4,8]{1,0:T(4,128)}, f32[4,8]{1,0:T(4,128)S(1)}, u32[]{:S(2)}) copy-start(f32[4,8]{1,0:T(4,128)S(1)} %div.230) | copy-start | bytes 388
  25.0 262.5 %copy-start.137 = (f32[4,8]{1,0:T(4,128)}, f32[4,8]{1,0:T(4,128)S(1)}, u32[]{:S(2)}) copy-start(f32[4,8]{1,0:T(4,128)S(1)} %rsqrt.93) | copy-start | bytes 388
  25.9 131.2 %copy-start.124 = (f32[4,256]{1,0:T(4,128)}, f32[4,256]{1,0:T(4,128)S(1)}, u32[]{:S(2)}) copy-start(f32[4,256]{1,0:T(4,128)S(1)} %div.221) | copy-start | bytes 12292
  26.6 97.2 %copy-start.119 = (f32[4,256]{1,0:T(4,128)}, f32[4,256]{1,0:T(4,128)S(1)}, u32[]{:S(2)}) copy-start(f32[4,256]{1,0:T(4,128)S(1)} %add.265) | copy-start | bytes 12292
  26.6 130.6 %copy-start.126 = (f32[4,256]{1,0:T(4,128)}, f32[4,256]{1,0:T(4,128)S(1)}, u32[]{:S(2)}) copy-start(f32[4,256]{1,0:T(4,128)S(1)} %rsqrt.90) | copy-start | bytes 12292
  129.0 79.0 %copy-start.105 = (f32[768]{0:T(1024)}, f32[768]{0:T(1024)S(1)}, u32[]{:S(2)}) copy-start(f32[768]{0:T(1024)S(1)} %mul.720) | copy-start | bytes 9220
  129.1 199.5 %copy-start.98 = (f32[768]{0:T(1024)}, f32[768]{0:T(1024)S(1)}, u32[]{:S(2)}) copy-start(f32[768]{0:T(1024)S(1)} %mul.771) | copy-start | bytes 9220
  129.2 158.3 %copy-start.113 = (f32[768]{0:T(1024)}, f32[768]{0:T(1024)S(1)}, u32[]{:S(2)}) copy-start(f32[768]{0:T(1024)S(1)} %mul.743) | copy-start | bytes 9220
  129.3 160.7 %copy-start.100 = (f32[768]{0:T(1024)}, f32[768]{0:T(1024)S(1)}, u32[]{:S(2)}) copy-start(f32[768]{0:T(1024)S(1)} %mul.737) | copy-start | bytes 9220
  130.7 53.5 %copy-start.142 = (f32[768]{0:T(1024)}, f32[768]{0:T(1024)S(1)}, u32[]{:S(2)}) copy-start(f32[768]{0:T(1024)S(1)} %mul.727) | copy-start | bytes 9220
  207.3 65.2 %copy-start.117 = (f32[4,256]{1,0:T(4,128)}, f32[4,256]{1,0:T(4,128)S(1)}, u32[]{:S(2)}) copy-start(f32[4,256]{1,0:T(4,128)S(1)} %multiply_reduce_fusion.9) | copy-start | bytes 12292
  207.3 82.6 %copy-start.109 = (f32[4,256]{1,0:T(4,128)}, f32[4,256]{1,0:T(4,128)S(1)}, u32[]{:S(2)}) copy-start(f32[4,256]{1,0:T(4,128)S(1)} %fusion.135) | copy-start | bytes 12292
  308.9 44.4 %copy-start.35 = (f32[4,8,768]{2,1,0:T(8,128)}, f32[4,8,768]{2,1,0:T(8,128)S(1)}, u32[]{:S(2)}) copy-start(f32[4,8,768]{2,1,0:T(8,128)S(1)} %get-tuple-element.118) | copy-start | bytes 294916
  335.1 20.5 %copy-start.94 = (f32[768]{0:T(1024)S(1)}, f32[768]{0:T(1024)}, u32[]{:S(2)}) copy-start(f32[768]{0:T(1024)} %mul.758) | copy-start | bytes 9220
  483.1 19.0 %slice-start.9 = ((s8[4718592]{0:T(1024)(128)(4,1)}), s8[4194304]{0:T(1024)(128)(4,1)S(1)}, s32[]{:S(2)}) async-start(s8[4718592]{0:T(1024)(128)(4,1)} %bitcast.430), calls=%async_computation.13 | async-start | bytes 8388608
  485.3 43.9 %copy-start.7 = (f32[4,256,768]{2,1,0:T(8,128)}, f32[4,256,768]{2,1,0:T(8,128)S(1)}, u32[]{:S(2)}) copy-start(f32[4,256,768]{2,1,0:T(8,128)S(1)} %get-tuple-element.64) | copy-start | bytes 9437188
  485.4 16.7 %copy-start.16 = (f32[4,256,768]{2,1,0:T(8,128)S(1)}, f32[4,256,768]{2,1,0:T(8,128)}, u32[]{:S(2)}) copy-start(f32[4,256,768]{2,1,0:T(8,128)} %copy-done.15) | copy-start | bytes 9437188
  485.4 16.7 %slice-start.10 = ((s8[4718592]{0:T(1024)(128)(4,1)}), s8[524288]{0:T(1024)(128)(4,1)S(1)}, s32[]{:S(2)}) async-start(s8[4718592]{0:T(1024)(128)(4,1)} %bitcast.430), calls=%async_computation.14 | async-start | bytes 1048576
  485.4 16.7 %copy-start.108 = (f32[4,256]{1,0:T(4,128)S(1)}, f32[4,256]{1,0:T(4,128)}, u32[]{:S(2)}) copy-start(f32[4,256]{1,0:T(4,128)} %copy-done.107) | copy-start | bytes 12292
  485.4 16.7 %copy-start.143 = (f32[768]{0:T(1024)S(1)}, f32[768]{0:T(1024)}, u32[]{:S(2)}) copy-start(f32[768]{0:T(1024)} %copy-done.142) | copy-start | bytes 9220
  485.4 16.7 %copy-start.149 = (f32[4,256]{1,0:T(4,128)S(1)}, f32[4,256]{1,0:T(4,128)}, u32[]{:S(2)}) copy-start(f32[4,256]{1,0:T(4,128)} %copy-done.148) | copy-start | bytes 12292
  502.1 15.7 %slice-start.11 = ((s8[6291456]{0:T(1024)(128)(4,1)}), s8[4194304]{0:T(1024)(128)(4,1)S(1)}, s32[]{:S(2)}) async-start(s8[6291456]{0:T(1024)(128)(4,1)} %bitcast.476), calls=%async_computation.15 | async-start | bytes 8388608
  536.8 17.4 %slice-start = ((s8[12582912]{0:T(1024)(128)(4,1)}), s8[4194304]{0:T(1024)(128)(4,1)S(1)}, s32[]{:S(2)}) async-start(s8[12582912]{0:T(1024)(128)(4,1)} %bitcast.357), calls=%async_computation.4 | async-start | bytes 8388608
  536.9 17.4 %slice-start.1 = ((s8[12582912]{0:T(1024)(128)(4,1)}), s8[4194304]{0:T(1024)(128)(4,1)S(1)}, s32[]{:S(2)}) async-start(s8[12582912]{0:T(1024)(128)(4,1)} %bitcast.357), calls=%async_computation.5 | async-start | bytes 8388608
  793.9 16.6 %copy-start.3 = (bf16[1024,768]{1,0:T(8,128)(2,1)S(1)}, bf16[1024,768]{1,0:T(8,128)(2,1)}, u32[]{:S(2)}) copy-start(bf16[1024,768]{1,0:T(8,128)(2,1)} %param.18) | copy-start | bytes 4718596
  (161 other events, 801.1 us)
Sparse Core Ops, SparseCore 0:
  12.8 107.6 all-gather.4
  123.3 145.2 all-gather.6
  422.4 22.5 reduce-scatter.3
